TPU v7x, 32 devices: a whole 2x2x4 slice. The times are simulated.
32 devices in a mesh: row: 4 (over z), col: 8 (over y, x, core).
Axes of the slice: x: 2, y: 2, z: 4, core: 2. Of those that a mesh axis runs over, the one named last changes fastest.
Arguments:
- tokens: bfloat16 [512, 8192], P('col', 'row'), may hold values from -6 to 6
- modality: int32 [512], P('row'), may hold values 0 or 1
- in_weight: bfloat16 [8192, 2, 28672], P('row', None, 'col'), may hold values from -0.0625 to 0.0625
- down_weight: bfloat16 [28672, 8192], P('col', 'row'), may hold values from -0.03125 to 0.03125
- d_mixed: bfloat16 [512, 8192], P('col', 'row'), may hold values from -6 to 6
Outputs:
- mixed: bfloat16 [512, 8192], P('col', 'row')
- d_down: bfloat16 [28672, 8192], P('col', 'row')
- d_in: bfloat16 [8192, 2, 28672], P('row', None, 'col')
- d_tokens: bfloat16 [512, 8192], P('col', 'row')
All inputs are finite; a program needn't handle non-finite values. No bound on the sum of `modality` on one device may be relied on, other than what follows from the above.
Results may differ from a plain program's by a relative error of at most 0.0049.
Values may be sent and summed in bfloat16 or wider, within the bound.
A program may use at most 192 MiB of HBM per device.

v0:
```python
import jax
import jax.numpy as jnp
from jax import lax
from jax.sharding import PartitionSpec as P


def swish_terms(projected, selected, width):
    gate_part = projected[:, :width]
    up_part = projected[:, width:]
    sigmoid_gate = jax.nn.sigmoid(gate_part)
    activated = gate_part * sigmoid_gate
    return (selected * activated * up_part).astype(jnp.bfloat16)


def grad_terms(projected, selected, d_hidden, width):
    gate_part = projected[:, :width]
    up_part = projected[:, width:]
    sigmoid_gate = jax.nn.sigmoid(gate_part)
    activated = gate_part * sigmoid_gate
    d_scaled = selected * d_hidden
    d_gate = d_scaled * up_part * (sigmoid_gate + gate_part * sigmoid_gate * (1.0 - sigmoid_gate))
    d_up = d_scaled * activated
    return jnp.concatenate([d_gate, d_up], 1).astype(jnp.bfloat16)


def per_device(tokens, modality, in_weight, down_weight, d_mixed):
    width = in_weight.shape[2]
    flat_in = in_weight.reshape(in_weight.shape[0], 2 * width)
    rows_all, cotangent_all = (
        lax.all_gather(tokens, "col", axis=0, tiled=True),
        lax.all_gather(d_mixed, "col", axis=0, tiled=True),
    )
    slab = rows_all
    projected = lax.psum_scatter(
        jnp.dot(slab, flat_in, preferred_element_type=jnp.float32),
        "row",
        scatter_dimension=0,
        tiled=True,
    )
    selected = (modality == 1).astype(jnp.float32)[:, None]
    hidden = swish_terms(projected, selected, width)
    hidden_all = lax.all_gather(hidden, "row", axis=0, tiled=True)
    slab = hidden_all
    mixed = lax.psum_scatter(
        jnp.dot(slab, down_weight, preferred_element_type=jnp.float32),
        "col",
        scatter_dimension=0,
        tiled=True,
    ).astype(jnp.bfloat16)
    d_down = jnp.einsum(
        "tf,td->fd", hidden_all, cotangent_all, preferred_element_type=jnp.float32
    ).astype(jnp.bfloat16)
    slab = cotangent_all
    d_hidden = lax.psum_scatter(
        jnp.einsum("td,fd->tf", slab, down_weight, preferred_element_type=jnp.float32),
        "row",
        scatter_dimension=0,
        tiled=True,
    )
    d_local = grad_terms(projected, selected, d_hidden, width)
    d_projected = lax.all_gather(d_local, "row", axis=0, tiled=True)
    d_in = jnp.einsum("td,tk->dk", rows_all, d_projected, preferred_element_type=jnp.float32)
    d_in = d_in.reshape(in_weight.shape).astype(jnp.bfloat16)
    slab = d_projected
    d_tokens = lax.psum_scatter(
        jnp.einsum("tk,dk->td", slab, flat_in, preferred_element_type=jnp.float32),
        "col",
        scatter_dimension=0,
        tiled=True,
    ).astype(jnp.bfloat16)
    return (mixed, d_down, d_in, d_tokens)


def solution(mesh):
    return jax.shard_map(
        per_device,
        mesh=mesh,
        in_specs=(
            P("col", "row"),
            P("row"),
            P("row", None, "col"),
            P("col", "row"),
            P("col", "row"),
        ),
        out_specs=(P("col", "row"), P("col", "row"), P("row", None, "col"), P("col", "row")),
        check_vma=False,
    )
```

profile of v0, /device:TPU:0, one launch (start us, length us, event | category | flops | bytes accessed | tf_op | source)
XLA Modules:
  0.0 800.1 jit_solution(11829566764625083146)
XLA Ops:
  7.2 0.0 all-gather.9.cloned.1.call-start
  7.2 0.7 all-gather.9.cloned.1.call-update
  7.9 0.0 all-gather.5.cloned.1.call-start
  7.9 0.7 all-gather.5.cloned.1.call-update
  8.6 0.0 reduce-scatter.9.cloned.1.call-start
  8.7 31.7 %all-gather.9.cloned.1.call-done = bf16[512,2048]{1,0:T(8,128)(2,1)} async-done(((bf16[64,2048]{1,0:T(8,128)(2,1)}), bf16[512,2048]{1,0:T(8,128)(2,1)}) %all-gather.9.cloned.1.call-update) | async-done | bytes 2097168 | tf_op jit(solution)/shard_map/all_gather | solution.py:31
  40.4 13.6 %fusion.2 = f32[512,3584]{1,0:T(8,128)} fusion(bf16[512,2048]{1,0:T(8,128)(2,1)} %all-gather.9.cloned.1.call-done, bf16[3584,2048]{1,0:T(8,128)(2,1)} %param.8), kind=kOutput, calls=%fused_computation.11 | convolution fusion | flops 7516192768 | bytes 24117248 | tf_op jit(solution)/shard_map/td,fd->tf/dot_general | solution.py:55
  54.0 0.0 reduce-scatter.9.cloned.1.call-update
  54.0 0.0 reduce-scatter.5.cloned.1.call-start
  54.1 20.9 %copy.10 = bf16[256,8,2,3584]{3,1,2,0:T(8,128)(2,1)} copy(bf16[256,8,2,3584]{3,2,1,0:T(2,128)(2,1)} %bitcast.17) | data formatting | bytes 58720256
  74.9 0.0 all-gather.5.cloned.1.call-done
  74.9 25.7 %fusion = f32[512,7168]{1,0:T(8,128)} fusion(bf16[512,2048]{1,0:T(8,128)(2,1)} %all-gather.5.cloned.1.call-done, bf16[2048,7168]{1,0:T(8,128)(2,1)} %bitcast.18), kind=kOutput, calls=%fused_computation.9 | convolution fusion | flops 15032385536 | bytes 46137344 | tf_op jit(solution)/shard_map/dot_general | solution.py:35
  100.6 0.0 copy-start
  100.6 0.0 reduce-scatter.5.cloned.1.call-update
  100.6 0.0 all-gather.7.cloned.1.call-start
  100.7 0.6 copy-done
  101.3 98.9 %reduce-scatter.9.cloned.1.call-done = f32[128,3584]{1,0:T(8,128)} async-done(((f32[512,3584]{1,0:T(8,128)}), f32[128,3584]{1,0:T(8,128)}) %reduce-scatter.9.cloned.1.call-update) | async-done | bytes 1835024 | tf_op jit(solution)/shard_map/reduce_scatter | solution.py:54
  200.2 249.1 %reduce-scatter.5.cloned.1.call-done = f32[128,7168]{1,0:T(8,128)} async-done(((f32[512,7168]{1,0:T(8,128)}), f32[128,7168]{1,0:T(8,128)}) %reduce-scatter.5.cloned.1.call-update) | async-done | bytes 3670032 | tf_op jit(solution)/shard_map/reduce_scatter | solution.py:34
  449.3 4.7 multiply_convert_fusion.1
  454.0 0.0 all-gather.7.cloned.1.call-update
  454.0 0.0 all-gather.11.cloned.1.call-start
  454.1 1.4 pad_maximum_fusion
  455.5 0.0 all-gather.11.cloned.1.call-update
  455.5 0.2 reduce-scatter.7.cloned.1.call-start
  455.8 71.5 %all-gather.7.cloned.1.call-done = bf16[512,3584]{1,0:T(8,128)(2,1)} async-done(((bf16[128,3584]{1,0:T(8,128)(2,1)}), bf16[512,3584]{1,0:T(8,128)(2,1)}) %all-gather.7.cloned.1.call-update) | async-done | bytes 3670032 | tf_op jit(solution)/shard_map/all_gather | solution.py:42
  527.3 13.4 %fusion.1 = f32[512,2048]{1,0:T(8,128)} fusion(bf16[512,3584]{1,0:T(8,128)(2,1)} %all-gather.7.cloned.1.call-done, bf16[3584,2048]{1,0:T(8,128)(2,1)} %param.8), kind=kOutput, calls=%fused_computation.10 | convolution fusion | flops 7516192768 | bytes 22544384 | tf_op jit(solution)/shard_map/dot_general | solution.py:45
  540.7 0.0 reduce-scatter.7.cloned.1.call-update
  540.8 0.0 reduce-scatter.11.cloned.1.call-start
  540.8 119.6 %all-gather.11.cloned.1.call-done = bf16[512,7168]{1,0:T(8,128)(2,1)} async-done(((bf16[128,7168]{1,0:T(8,128)(2,1)}), bf16[512,7168]{1,0:T(8,128)(2,1)}) %all-gather.11.cloned.1.call-update) | async-done | bytes 7340048 | tf_op jit(solution)/shard_map/all_gather | solution.py:61
  660.4 22.3 %fusion.3 = f32[512,2048]{1,0:T(8,128)} fusion(bf16[512,7168]{1,0:T(8,128)(2,1)} %all-gather.11.cloned.1.call-done, bf16[2048,7168]{1,0:T(8,128)(2,1)} %bitcast.19), kind=kOutput, calls=%fused_computation.12 | convolution fusion | flops 15032385536 | bytes 40894464 | tf_op jit(solution)/shard_map/tk,dk->td/dot_general | solution.py:66
  682.7 0.0 slice-start
  682.7 0.0 reduce-scatter.11.cloned.1.call-update
  682.7 0.0 slice-start.1
  682.7 14.1 %convolution_convert_fusion.1 = bf16[3584,2048]{1,0:T(8,128)(2,1)} fusion(bf16[512,3584]{1,0:T(8,128)(2,1)} %all-gather.7.cloned.1.call-done, bf16[512,2048]{1,0:T(8,128)(2,1)} %all-gather.9.cloned.1.call-done), kind=kOutput, calls=%fused_computation.1 | convolution fusion | flops 7523532800 | bytes 20447232 | tf_op jit(solution)/shard_map/tf,td->fd/dot_general | solution.py:50
  696.8 0.0 slice-done
  696.8 0.0 slice-done.1
  696.8 20.8 %convolution_convert_fusion = bf16[7168,2048]{1,0:T(8,128)(2,1)} fusion(bf16[512,7168]{1,0:T(8,128)(2,1)S(1)} %bitcast.22, bf16[512,2048]{1,0:T(8,128)(2,1)} %all-gather.5.cloned.1.call-done), kind=kOutput, calls=%fused_computation | convolution fusion | flops 15047065600 | bytes 38797312 | tf_op jit(solution)/shard_map/td,tk->dk/dot_general | solution.py:62
  717.5 72.2 %copy.9 = bf16[2048,2,3584]{2,1,0:T(2,128)(2,1)} copy(bf16[2048,2,3584]{0,2,1:T(8,128)(2,1)} %bitcast.20) | data formatting | bytes 58720256
  789.7 0.0 reduce-scatter.7.cloned.1.call-done
  789.7 1.8 convert_element_type.27
  791.5 0.0 reduce-scatter.11.cloned.1.call-done
  791.5 1.8 convert_element_type.32
  (2 shorter events, 0.0 us)
Async XLA Ops:
  7.2 33.2 %all-gather.9.cloned.1.call-start = ((), (), s32[]{:S(2)}) async-start(), calls=%async_computation.8 | async-start | bytes 2359296 | tf_op jit(solution)/shard_map/all_gather | solution.py:31
  7.9 67.0 %all-gather.5.cloned.1.call-start = ((), (), s32[]{:S(2)}) async-start(), calls=%async_computation.4 | async-start | bytes 2359296 | tf_op jit(solution)/shard_map/all_gather | solution.py:30
  8.6 191.6 %reduce-scatter.9.cloned.1.call-start = ((), (), s32[]{:S(2)}) async-start(), calls=%async_computation.9 | async-start | bytes 9175040 | tf_op jit(solution)/shard_map/reduce_scatter | solution.py:54
  54.0 395.3 %reduce-scatter.5.cloned.1.call-start = ((), (), s32[]{:S(2)}) async-start(), calls=%async_computation.5 | async-start | bytes 18350080 | tf_op jit(solution)/shard_map/reduce_scatter | solution.py:34
  100.6 0.7 copy-start
  100.6 426.7 %all-gather.7.cloned.1.call-start = ((), (), s32[]{:S(2)}) async-start(), calls=%async_computation.6 | async-start | bytes 4587520 | tf_op jit(solution)/shard_map/all_gather | solution.py:42
  454.0 206.3 %all-gather.11.cloned.1.call-start = ((), (), s32[]{:S(2)}) async-start(), calls=%async_computation.10 | async-start | bytes 9175040 | tf_op jit(solution)/shard_map/all_gather | solution.py:61
  455.5 334.2 %reduce-scatter.7.cloned.1.call-start = ((), (), s32[]{:S(2)}) async-start(), calls=%async_computation.7 | async-start | bytes 4718592 | tf_op jit(solution)/shard_map/reduce_scatter | solution.py:44
  540.8 250.8 %reduce-scatter.11.cloned.1.call-start = ((), (), s32[]{:S(2)}) async-start(), calls=%async_computation.11 | async-start | bytes 4718592 | tf_op jit(solution)/shard_map/reduce_scatter | solution.py:65
  682.7 14.1 %slice-start = ((s8[7340032]{0:T(1024)(128)(4,1)}), s8[3145728]{0:T(1024)(128)(4,1)S(1)}, s32[]{:S(2)}) async-start(s8[7340032]{0:T(1024)(128)(4,1)} %bitcast.21), calls=%async_computation.12 | async-start | bytes 6291456
  682.7 14.1 %slice-start.1 = ((s8[7340032]{0:T(1024)(128)(4,1)}), s8[4194304]{0:T(1024)(128)(4,1)S(1)}, s32[]{:S(2)}) async-start(s8[7340032]{0:T(1024)(128)(4,1)} %bitcast.21), calls=%async_computation.13 | async-start | bytes 8388608
Sparse Core Ops, SparseCore 0:
  9.9 30.4 all-gather.8
  42.3 27.7 all-gather.4
  72.4 127.7 reduce-scatter.8
  203.0 246.2 reduce-scatter.4
  454.2 73.1 all-gather.6
  529.3 131.0 all-gather.10
  663.7 49.3 reduce-scatter.6
  716.5 51.1 reduce-scatter.10
where the time goes:
time: 802 us; the launch traced here: 800 us
  waiting for transfers between devices  572 us (71%)
  matrix products  110 us (14%)
  local copies, waits for them, and re-layouts  93.7 us (12%)
  between operations  14.2 us (2%)
  other arithmetic  9.7 us (1%)
    reduce_scatter x1, waiting for transfers between devices, per_device(): lax.psum_scatter(jnp.dot(slab, flat_in, preferred_element_type=jnp.float3...  249 us
    all_gather x1, waiting for transfers between devices, per_device(): d_projected = lax.all_gather(d_local, 'row', axis=0, tiled=True)  120 us
    reduce_scatter x1, waiting for transfers between devices, per_device(): lax.psum_scatter(jnp.einsum('td,fd->tf', slab, down_weight, preferred_ele...  98.9 us
    unnamed x8, local copies, waits for them, and re-layouts  93.7 us
    all_gather x1, waiting for transfers between devices, per_device(): hidden_all = lax.all_gather(hidden, 'row', axis=0, tiled=True)  71.5 us
    all_gather x1, waiting for transfers between devices, per_device(): lax.all_gather(d_mixed, 'col', axis=0, tiled=True)  31.7 us
    dot_general x1, matrix products, per_device(): jnp.dot(slab, flat_in, preferred_element_type=jnp.float32)  25.7 us
    dot_general x1, matrix products, per_device(): jnp.einsum('tk,dk->td', slab, flat_in, preferred_element_type=jnp.float32)  22.3 us
  transfers between devices with their start and end apart: 8, of which 5 were waited for; matrix products, arithmetic and copies ran while one was open for 26% of the time, Pallas kernels for 0%

commit v1 on v0

v1 whole, which is shorter than its diff:
```python
import jax
import jax.numpy as jnp
from jax import lax
from jax.sharding import PartitionSpec as P


def exchange(partial, axis):
    count = lax.axis_size(axis)
    me = lax.axis_index(axis)
    rows = partial.shape[0] // count
    received = []
    for shift in range(1, count):
        start = lax.rem(me + shift, count) * rows
        block = lax.dynamic_slice_in_dim(partial, start, rows, 0).astype(jnp.bfloat16)
        moves = [(i, (i + shift) % count) for i in range(count)]
        received.append(lax.ppermute(block, axis, moves))
    total = lax.dynamic_slice_in_dim(partial, me * rows, rows, 0)
    for block in received:
        total = total + block.astype(jnp.float32)
    return total


def block_terms(rows, cotangents, in_weight, down_weight, spread):
    width = in_weight.shape[2]
    flat_in = in_weight.reshape(in_weight.shape[0], 2 * width)
    d_hidden = exchange(
        jnp.einsum("td,fd->tf", cotangents, down_weight, preferred_element_type=jnp.float32), "row"
    )
    projected = exchange(jnp.dot(rows, flat_in, preferred_element_type=jnp.float32), "row")
    gate_part = projected[:, :width]
    up_part = projected[:, width:]
    sigmoid_gate = jax.nn.sigmoid(gate_part)
    activated = gate_part * sigmoid_gate
    hidden = (activated * up_part).astype(jnp.bfloat16)
    d_gate = d_hidden * up_part * (sigmoid_gate + gate_part * sigmoid_gate * (1.0 - sigmoid_gate))
    d_local = jnp.concatenate([d_gate, d_hidden * activated], 1).astype(jnp.bfloat16)
    hidden_all = lax.all_gather(hidden, "row", axis=0, tiled=True)
    d_projected = lax.all_gather(d_local, "row", axis=0, tiled=True)
    mixed = lax.psum_scatter(
        jnp.dot(spread(hidden_all), down_weight, preferred_element_type=jnp.float32),
        "col",
        scatter_dimension=0,
        tiled=True,
    ).astype(jnp.bfloat16)
    d_down = jnp.einsum(
        "tf,td->fd", hidden_all, cotangents, preferred_element_type=jnp.float32
    ).astype(jnp.bfloat16)
    d_tokens = lax.psum_scatter(
        jnp.einsum("tk,dk->td", spread(d_projected), flat_in, preferred_element_type=jnp.float32),
        "col",
        scatter_dimension=0,
        tiled=True,
    ).astype(jnp.bfloat16)
    d_in = jnp.einsum("td,tk->dk", rows, d_projected, preferred_element_type=jnp.float32)
    d_in = lax.optimization_barrier(d_in.astype(jnp.bfloat16))
    return (mixed, d_down, d_in.reshape(in_weight.shape), d_tokens)


def per_device(tokens, modality, in_weight, down_weight, d_mixed):
    cotangent_all = lax.all_gather(d_mixed, "col", axis=0, tiled=True)
    rows_all = lax.all_gather(tokens, "col", axis=0, tiled=True)
    chosen = lax.all_gather(modality, "row", axis=0, tiled=True) == 1
    total = chosen.shape[0]
    place = jnp.cumsum(chosen.astype(jnp.int32)) - 1
    packed = total * 5 // 8

    def packed_form(rows, cotangents, w_in, w_down):
        pick = (chosen[None, :] & (place[None, :] == jnp.arange(packed)[:, None])).astype(jnp.bfloat16)
        take = lambda x: jnp.dot(pick, x, preferred_element_type=jnp.float32).astype(jnp.bfloat16)
        spread = lambda x: jnp.einsum(
            "ct,cf->tf", pick, x, preferred_element_type=jnp.float32
        ).astype(jnp.bfloat16)
        return block_terms(take(rows), take(cotangents), w_in, w_down, spread)

    def whole_form(rows, cotangents, w_in, w_down):
        keep = chosen[:, None].astype(jnp.bfloat16)
        return block_terms(rows * keep, cotangents * keep, w_in, w_down, lambda x: x)

    return lax.cond(
        place[-1] < packed, packed_form, whole_form, rows_all, cotangent_all, in_weight, down_weight
    )


def solution(mesh):
    return jax.shard_map(
        per_device,
        mesh=mesh,
        in_specs=(
            P("col", "row"),
            P("row"),
            P("row", None, "col"),
            P("col", "row"),
            P("col", "row"),
        ),
        out_specs=(P("col", "row"), P("col", "row"), P("row", None, "col"), P("col", "row")),
        check_vma=False,
    )
```

time: 802 us -> 557 us (0.69); the launches traced: 800 us -> 547 us
  waiting for transfers between devices: 572 us -> 241 us
  starting transfers between devices: 0.5 us -> 58.7 us
  blocking collectives: 0 us -> 12.8 us
    reduce_scatter x4 -> x2, waiting for transfers between devices: 348 us -> 0.02 us  [the longest x1 0.02 us: block_terms(): lax.psum_scatter(jnp.einsum('tk,dk->td', spread(d_projected), flat_in, pr...]
    ppermute x0 -> x6, waiting for transfers between devices: none -> 76.4 us  [exchange(): received.append(lax.ppermute(block, axis, moves))]
    unnamed x8 -> x33, local copies, waits for them, and re-layouts: 93.7 us -> 30.9 us
    reshape x0 -> x1, local copies, waits for them, and re-layouts: none -> 62.7 us  [block_terms(): return (mixed, d_down, d_in.reshape(in_weight.shape), d_tokens)]
    all_gather x4, waiting for transfers between devices: 223 us -> 163 us  [the longest x1 70.2 us: block_terms(): d_projected = lax.all_gather(d_local, 'row', axis=0, tiled=True)]
    ppermute x0 -> x6, starting transfers between devices: none -> 58 us  [exchange(): received.append(lax.ppermute(block, axis, moves))]
    all_gather x0 -> x1, blocking collectives: none -> 12.8 us  [per_device(): chosen = lax.all_gather(modality, 'row', axis=0, tiled=True) == 1]
    dot_general x6 -> x9, matrix products: 110 us -> 104 us  [the longest x1 22 us: block_terms(): jnp.einsum('tk,dk->td', spread(d_projected), flat_in, preferred_element_t...]
  transfers between devices with their start and end apart: 8 -> 12, of which waited for: 5 -> 7; matrix products, arithmetic and copies ran while one was open for 26% -> 29% of each run, Pallas kernels for 0% -> 0%
where the time goes in v1:
time: 557 us; the launch traced here: 547 us
  waiting for transfers between devices  241 us (43%)
  matrix products  104 us (19%)
  local copies, waits for them, and re-layouts  97.4 us (17%)
  starting transfers between devices  58.7 us (11%)
  between operations  15.3 us (3%)
  blocking collectives  12.8 us (2%)
  other arithmetic  9.84 us (2%)
  loops' own time  7.87 us (1%)
    ppermute x6, waiting for transfers between devices, exchange(): received.append(lax.ppermute(block, axis, moves))  76.4 us
    all_gather x1, waiting for transfers between devices, block_terms(): d_projected = lax.all_gather(d_local, 'row', axis=0, tiled=True)  70.2 us
    reshape x1, local copies, waits for them, and re-layouts, block_terms(): return (mixed, d_down, d_in.reshape(in_weight.shape), d_tokens)  62.7 us
    ppermute x6, starting transfers between devices, exchange(): received.append(lax.ppermute(block, axis, moves))  58 us
    all_gather x1, waiting for transfers between devices, block_terms(): hidden_all = lax.all_gather(hidden, 'row', axis=0, tiled=True)  45.8 us
    unnamed x33, local copies, waits for them, and re-layouts  30.9 us
    all_gather x1, waiting for transfers between devices, per_device(): cotangent_all = lax.all_gather(d_mixed, 'col', axis=0, tiled=True)  29.7 us
    dot_general x1, matrix products, block_terms(): jnp.einsum('tk,dk->td', spread(d_projected), flat_in, preferred_element_t...  22 us
  transfers between devices with their start and end apart: 12, of which 7 were waited for; matrix products, arithmetic and copies ran while one was open for 29% of the time, Pallas kernels for 0%

profile of v1, /device:TPU:0, one launch (start us, length us, event | category | flops | bytes accessed | tf_op | source)
XLA Modules:
  0.0 546.8 jit_solution(8745290950249474344)
XLA Ops:
  7.2 0.7 all-gather.16.cloned.1.call-update
  7.9 0.7 all-gather.18.cloned.1.call-update
  8.7 12.8 %all-gather = s32[4,1,128]{2,1,0:T(1,128)S(1)} all-gather(s32[1,1,128]{2,1,0:T(1,128)} %bitcast.47), channel_id=1, replica_groups=mesh['row'=4,'col'=8] {'row'}, dimensions={0}, use_global_device_ids=true | all-gather | bytes 2560 | tf_op jit(solution)/shard_map/all_gather | solution.py:62
  21.5 0.3 reduce-window.9
  21.8 0.1 slice.22
  21.9 0.1 slice_reduce_fusion
  22.1 0.6 slice.24
  23.3 17.1 %all-gather.16.cloned.1.call-done = bf16[512,2048]{1,0:T(8,128)(2,1)} async-done(((bf16[64,2048]{1,0:T(8,128)(2,1)}), bf16[512,2048]{1,0:T(8,128)(2,1)}) %all-gather.16.cloned.1.call-update) | async-done | bytes 2097168 | tf_op jit(solution)/shard_map/all_gather | solution.py:61
  40.4 29.7 %all-gather.18.cloned.1.call-done = bf16[512,2048]{1,0:T(8,128)(2,1)} async-done(((bf16[64,2048]{1,0:T(8,128)(2,1)}), bf16[512,2048]{1,0:T(8,128)(2,1)}) %all-gather.18.cloned.1.call-update) | async-done | bytes 2097168 | tf_op jit(solution)/shard_map/all_gather | solution.py:60
  70.1 468.5 %conditional.4 = (bf16[3584,2048]{1,0:T(8,128)(2,1)}, bf16[2048,2,3584]{2,1,0:T(2,128)(2,1)}, bf16[64,2048]{1,0:T(8,128)(2,1)S(1)}, bf16[64,2048]{1,0:T(8,128)(2,1)S(1)}) conditional(s32[]{:T(128)} %bitcast.3, (pred[512]{0:T(512)(128)(4,1)S(1)}, bf16[512,2048]{1,0:T(8,128)(2,1)}, bf16[2048,2,3584]{2,1,0:T(2,128)(2,1)}, bf16[512,2048]{1,0:T(8,128)(2,1)}, ...), branch_computations={%region_2.5_spmd, %region_5.8_spmd} | conditional | flops 67683221504 | bytes 523648416
  77.5 20.9 %copy.10 = bf16[256,8,2,3584]{3,1,2,0:T(8,128)(2,1)} copy(bf16[256,8,2,3584]{3,2,1,0:T(2,128)(2,1)} %bitcast.40) | data formatting | bytes 58720256
  98.4 0.8 convolution_convert_fusion.5
  99.2 1.1 copy-done.16
  100.3 14.7 %fusion.34 = f32[320,7168]{1,0:T(8,128)S(1)} fusion(bf16[320,2048]{1,0:T(8,128)(2,1)S(1)} %convolution_convert_fusion.5, bf16[2048,7168]{1,0:T(8,128)(2,1)} %bitcast.41), kind=kOutput, calls=%fused_computation.63 | convolution fusion | flops 9395240960 | bytes 39845888 | tf_op jit(solution)/shard_map/cond/branch_1_fun/dot_general | solution.py:29
  115.0 3.6 copy-done
  118.6 1.8 dynamic-slice_convert_fusion.8
  120.4 1.5 collective-permute-start.6
  121.9 2.3 collective-permute-start.8
  124.3 0.6 collective-permute-start.7
  124.9 2.0 convolution_convert_fusion.4
  126.8 8.6 %fusion.36 = f32[320,3584]{1,0:T(8,128)S(1)} fusion(bf16[320,2048]{1,0:T(8,128)(2,1)} %convolution_convert_fusion.4, bf16[3584,2048]{1,0:T(8,128)(2,1)} %get-tuple-element.49), kind=kOutput, calls=%fused_computation.65 | convolution fusion | flops 4697620480 | bytes 20578304 | tf_op jit(solution)/shard_map/cond/branch_1_fun/td,fd->tf/dot_general | solution.py:27
  135.4 2.1 copy-done.2
  137.5 1.3 dynamic-slice_convert_fusion.11
  138.8 1.5 collective-permute-start.9
  140.3 2.4 collective-permute-start.11
  142.6 8.1 %collective-permute-done.6 = bf16[80,7168]{1,0:T(8,128)(2,1)} collective-permute-done((bf16[80,7168]{1,0:T(8,128)(2,1)}, bf16[80,7168]{1,0:T(8,128)(2,1)}, u32[]{:S(2)}, u32[]{:S(2)}) %collective-permute-start.6) | collective-permute-done | bytes 1146912 | tf_op jit(solution)/shard_map/cond/branch_1_fun/ppermute | solution.py:16
  150.7 49.7 %collective-permute-start.10 = (bf16[80,3584]{1,0:T(8,128)(2,1)}, bf16[80,3584]{1,0:T(8,128)(2,1)S(1)}, u32[]{:S(2)}, u32[]{:S(2)}) collective-permute-start(bf16[80,3584]{1,0:T(8,128)(2,1)} %get-tuple-element.86), channel_id=1, source_target_pairs={{0,16},{8,24},{16,0},{24,8},{1,17},{9,25},{17,1},{25,9},{2,18},{10... | collective-permute-start | bytes 1720328 | tf_op jit(solution)/shard_map/cond/branch_1_fun/ppermute | solution.py:16
  200.4 47.9 %collective-permute-done.7 = bf16[80,7168]{1,0:T(8,128)(2,1)} collective-permute-done((bf16[80,7168]{1,0:T(8,128)(2,1)S(1)}, bf16[80,7168]{1,0:T(8,128)(2,1)}, u32[]{:S(2)}, u32[]{:S(2)}) %collective-permute-start.7) | collective-permute-done | bytes 1146912 | tf_op jit(solution)/shard_map/cond/branch_1_fun/ppermute | solution.py:16
  248.4 3.2 convert_add_fusion.2
  251.5 0.8 copy-done.3
  252.3 20.4 %collective-permute-done.10 = bf16[80,3584]{1,0:T(8,128)(2,1)S(1)} collective-permute-done((bf16[80,3584]{1,0:T(8,128)(2,1)}, bf16[80,3584]{1,0:T(8,128)(2,1)S(1)}, u32[]{:S(2)}, u32[]{:S(2)}) %collective-permute-start.10) | collective-permute-done | bytes 573472 | tf_op jit(solution)/shard_map/cond/branch_1_fun/ppermute | solution.py:16
  272.7 3.0 multiply_convert_fusion.4
  275.8 1.1 pad_maximum_fusion.1
  276.9 0.3 reduce-scatter.9.cloned.1.call-start
  277.2 45.8 %all-gather.12.cloned.1.call-done = bf16[320,3584]{1,0:T(8,128)(2,1)} async-done(((bf16[80,3584]{1,0:T(8,128)(2,1)}), bf16[320,3584]{1,0:T(8,128)(2,1)}) %all-gather.12.cloned.1.call-update) | async-done | bytes 2293776 | tf_op jit(solution)/shard_map/cond/branch_1_fun/all_gather | solution.py:37
  323.0 17.5 %fusion.11 = f32[512,2048]{1,0:T(8,128)} fusion(bf16[3584,2048]{1,0:T(8,128)(2,1)} %get-tuple-element.49, bf16[320,3584]{1,0:T(8,128)(2,1)} %all-gather.12.cloned.1.call-done, s32[512]{0:T(512)S(1)} %copy-done.9, pred[512]{0:T(512)(128)(4,1)S(1)} %copy-done.7), kind=kOutput, calls=%fused_computation.29 | convolution fusion | flops 8692760576 | bytes 21170688 | tf_op jit(solution)/shard_map/cond/branch_1_fun/dot_general | solution.py:40
  340.5 0.3 reduce-scatter.11.cloned.1.call-start
  340.8 70.2 %all-gather.14.cloned.1.call-done = bf16[320,7168]{1,0:T(8,128)(2,1)} async-done(((bf16[80,7168]{1,0:T(8,128)(2,1)}), bf16[320,7168]{1,0:T(8,128)(2,1)}) %all-gather.14.cloned.1.call-update) | async-done | bytes 4587536 | tf_op jit(solution)/shard_map/cond/branch_1_fun/all_gather | solution.py:38
  411.0 6.6 %convolution_convert_fusion.2.clone.4 = bf16[512,7168]{1,0:T(8,128)(2,1)S(1)} fusion(bf16[320,7168]{1,0:T(8,128)(2,1)} %all-gather.14.cloned.1.call-done, s32[512]{0:T(512)S(1)} %copy-done.9, pred[512]{0:T(512)(128)(4,1)S(1)} %copy-done.7), kind=kOutput, calls=%fused_computation.27.clone.clone.clone.1 | convolution fusion | flops 2352807936 | bytes 11930112 | tf_op jit(solution)/shard_map/cond/branch_1_fun/ct,cf->tf/dot_general | solution.py:70
  417.6 22.0 %fusion.12 = f32[512,2048]{1,0:T(8,128)} fusion(bf16[2048,7168]{1,0:T(8,128)(2,1)} %bitcast.42, bf16[512,7168]{1,0:T(8,128)(2,1)S(1)} %convolution_convert_fusion.2.clone.4), kind=kOutput, calls=%fused_computation.36 | convolution fusion | flops 15032385536 | bytes 40894464 | tf_op jit(solution)/shard_map/cond/branch_1_fun/tk,dk->td/dot_general | solution.py:49
  439.6 1.6 copy-done.10
  441.3 12.6 %fusion.35 = bf16[3584,2048]{1,0:T(8,128)(2,1)} fusion(bf16[320,3584]{1,0:T(8,128)(2,1)S(1)} %copy-done.10, bf16[320,2048]{1,0:T(8,128)(2,1)} %convolution_convert_fusion.4), kind=kOutput, calls=%fused_computation.64 | convolution fusion | flops 4697620480 | bytes 18284544 | tf_op jit(solution)/shard_map/cond/branch_1_fun/tf,td->fd/dot_general | solution.py:45
  453.9 19.5 %convolution_convert_fusion.1 = bf16[2048,7168]{1,0:T(8,128)(2,1)} fusion(bf16[320,2048]{1,0:T(8,128)(2,1)S(1)} %copy-done.17, bf16[320,7168]{1,0:T(8,128)(2,1)S(1)} %bitcast.49), kind=kOutput, calls=%fused_computation.26 | convolution fusion | flops 9409921024 | bytes 35258368 | tf_op jit(solution)/shard_map/cond/branch_1_fun/td,tk->dk/dot_general | solution.py:54
  473.4 62.7 %reshape.42 = bf16[2048,2,3584]{2,1,0:T(2,128)(2,1)} reshape(bf16[2048,7168]{1,0:T(8,128)(2,1)} %convolution_convert_fusion.1) | data formatting | bytes 58720256 | tf_op jit(solution)/shard_map/cond/branch_1_fun/reshape | solution.py:56
  536.1 1.1 convert_element_type.146
  537.2 1.1 convert_element_type.148
  538.6 0.7 copy-done.4
  539.3 0.1 copy-done.5
  (43 shorter events, 0.5 us)
Async XLA Ops:
  7.2 33.2 %all-gather.16.cloned.1.call-start = ((), (), s32[]{:S(2)}) async-start(), calls=%async_computation.12 | async-start | bytes 2359296 | tf_op jit(solution)/shard_map/all_gather | solution.py:61
  7.9 62.2 %all-gather.18.cloned.1.call-start = ((), (), s32[]{:S(2)}) async-start(), calls=%async_computation.13 | async-start | bytes 2359296 | tf_op jit(solution)/shard_map/all_gather | solution.py:60
  77.4 47.5 %copy-start.6 = (pred[512]{0:T(512)(128)(4,1)}, pred[512]{0:T(512)(128)(4,1)S(1)}, u32[]{:S(2)}) copy-start(pred[512]{0:T(512)(128)(4,1)S(1)} %get-tuple-element.44) | copy-start | bytes 1540
  77.4 47.5 %copy-start.8 = (s32[512]{0:T(512)}, s32[512]{0:T(512)S(1)}, u32[]{:S(2)}) copy-start(s32[512]{0:T(512)S(1)} %get-tuple-element.45) | copy-start | bytes 6148
  77.4 245.6 %all-gather.12.cloned.1.call-start = ((), (), s32[]{:S(2)}) async-start(), calls=%async_computation.8 | async-start | bytes 2867200 | tf_op jit(solution)/shard_map/cond/branch_1_fun/all_gather | solution.py:37
  77.5 20.9 %copy-start.13 = (bf16[512,2048]{1,0:T(8,128)(2,1)S(1)}, bf16[512,2048]{1,0:T(8,128)(2,1)}, u32[]{:S(2)}) copy-start(bf16[512,2048]{1,0:T(8,128)(2,1)} %get-tuple-element.46) | copy-start | bytes 6291460
  99.2 1.1 copy-start.16
  115.0 3.7 copy-start
  118.6 6.2 %copy-start.15 = (bf16[512,2048]{1,0:T(8,128)(2,1)S(1)}, bf16[512,2048]{1,0:T(8,128)(2,1)}, u32[]{:S(2)}) copy-start(bf16[512,2048]{1,0:T(8,128)(2,1)} %get-tuple-element.48) | copy-start | bytes 6291460
  120.4 30.3 %collective-permute-start.6 = (bf16[80,7168]{1,0:T(8,128)(2,1)}, bf16[80,7168]{1,0:T(8,128)(2,1)}, u32[]{:S(2)}, u32[]{:S(2)}) collective-permute-start(bf16[80,7168]{1,0:T(8,128)(2,1)} %get-tuple-element.79), channel_id=1, source_target_pairs={{0,8},{8,16},{16,24},{24,0},{1,9},{9,17},{17,25},{25,1},{2,10},{10... | collective-permute-start | bytes 3440648 | tf_op jit(solution)/shard_map/cond/branch_1_fun/ppermute | solution.py:16
  121.9 78.5 %collective-permute-start.8 = (bf16[80,7168]{1,0:T(8,128)(2,1)}, bf16[80,7168]{1,0:T(8,128)(2,1)}, u32[]{:S(2)}, u32[]{:S(2)}) collective-permute-start(bf16[80,7168]{1,0:T(8,128)(2,1)} %get-tuple-element.80), channel_id=1, source_target_pairs={{0,24},{8,0},{16,8},{24,16},{1,25},{9,1},{17,9},{25,17},{2,26},{10... | collective-permute-start | bytes 3440648 | tf_op jit(solution)/shard_map/cond/branch_1_fun/ppermute | solution.py:16
  124.3 124.1 %collective-permute-start.7 = (bf16[80,7168]{1,0:T(8,128)(2,1)S(1)}, bf16[80,7168]{1,0:T(8,128)(2,1)}, u32[]{:S(2)}, u32[]{:S(2)}) collective-permute-start(bf16[80,7168]{1,0:T(8,128)(2,1)S(1)} %get-tuple-element.81), channel_id=1, source_target_pairs={{0,16},{8,24},{16,0},{24,8},{1,17},{9,25},{17,1},{25,9},{2,18},{10... | collective-permute-start | bytes 3440648 | tf_op jit(solution)/shard_map/cond/branch_1_fun/ppermute | solution.py:16
  135.4 2.1 copy-start.2
  138.8 112.7 %collective-permute-start.9 = (bf16[80,3584]{1,0:T(8,128)(2,1)}, bf16[80,3584]{1,0:T(8,128)(2,1)S(1)}, u32[]{:S(2)}, u32[]{:S(2)}) collective-permute-start(bf16[80,3584]{1,0:T(8,128)(2,1)} %get-tuple-element.84), channel_id=1, source_target_pairs={{0,8},{8,16},{16,24},{24,0},{1,9},{9,17},{17,25},{25,1},{2,10},{10... | collective-permute-start | bytes 1720328 | tf_op jit(solution)/shard_map/cond/branch_1_fun/ppermute | solution.py:16
  140.3 111.3 %collective-permute-start.11 = (bf16[80,3584]{1,0:T(8,128)(2,1)}, bf16[80,3584]{1,0:T(8,128)(2,1)S(1)}, u32[]{:S(2)}, u32[]{:S(2)}) collective-permute-start(bf16[80,3584]{1,0:T(8,128)(2,1)} %get-tuple-element.85), channel_id=1, source_target_pairs={{0,24},{8,0},{16,8},{24,16},{1,25},{9,1},{17,9},{25,17},{2,26},{10... | collective-permute-start | bytes 1720328 | tf_op jit(solution)/shard_map/cond/branch_1_fun/ppermute | solution.py:16
  150.7 122.0 %collective-permute-start.10 = (bf16[80,3584]{1,0:T(8,128)(2,1)}, bf16[80,3584]{1,0:T(8,128)(2,1)S(1)}, u32[]{:S(2)}, u32[]{:S(2)}) collective-permute-start(bf16[80,3584]{1,0:T(8,128)(2,1)} %get-tuple-element.86), channel_id=1, source_target_pairs={{0,16},{8,24},{16,0},{24,8},{1,17},{9,25},{17,1},{25,9},{2,18},{10... | collective-permute-start | bytes 1720328 | tf_op jit(solution)/shard_map/cond/branch_1_fun/ppermute | solution.py:16
  251.5 0.8 copy-start.3
  275.7 47.3 %copy-start.7 = (pred[512]{0:T(512)(128)(4,1)S(1)}, pred[512]{0:T(512)(128)(4,1)}, u32[]{:S(2)}) copy-start(pred[512]{0:T(512)(128)(4,1)} %copy-done.6) | copy-start | bytes 1540
  275.7 47.3 %copy-start.9 = (s32[512]{0:T(512)S(1)}, s32[512]{0:T(512)}, u32[]{:S(2)}) copy-start(s32[512]{0:T(512)} %copy-done.8) | copy-start | bytes 6148
  275.8 135.3 %all-gather.14.cloned.1.call-start = ((), (), s32[]{:S(2)}) async-start(), calls=%async_computation.9 | async-start | bytes 5734400 | tf_op jit(solution)/shard_map/cond/branch_1_fun/all_gather | solution.py:38
  276.9 259.1 %reduce-scatter.9.cloned.1.call-start = ((), (), s32[]{:S(2)}) async-start(), calls=%async_computation.10 | async-start | bytes 4718592 | tf_op jit(solution)/shard_map/cond/branch_1_fun/reduce_scatter | solution.py:39
  340.5 196.6 %reduce-scatter.11.cloned.1.call-start = ((), (), s32[]{:S(2)}) async-start(), calls=%async_computation.11 | async-start | bytes 4718592 | tf_op jit(solution)/shard_map/cond/branch_1_fun/reduce_scatter | solution.py:48
  439.6 1.6 copy-start.10
  439.6 14.2 %slice-start = ((s8[4587520]{0:T(1024)(128)(4,1)}), s8[393216]{0:T(1024)(128)(4,1)S(1)}, s32[]{:S(2)}) async-start(s8[4587520]{0:T(1024)(128)(4,1)} %bitcast.48), calls=%async_computation.14 | async-start | bytes 786432
  441.3 12.6 %slice-start.1 = ((s8[4587520]{0:T(1024)(128)(4,1)}), s8[4194304]{0:T(1024)(128)(4,1)S(1)}, s32[]{:S(2)}) async-start(s8[4587520]{0:T(1024)(128)(4,1)} %bitcast.48), calls=%async_computation.15 | async-start | bytes 8388608
  441.3 12.6 %copy-start.17 = (bf16[320,2048]{1,0:T(8,128)(2,1)S(1)}, bf16[320,2048]{1,0:T(8,128)(2,1)}, u32[]{:S(2)}) copy-start(bf16[320,2048]{1,0:T(8,128)(2,1)} %copy-done.16) | copy-start | bytes 3932164
  538.6 0.7 copy-start.4
  538.6 0.8 copy-start.5
Sparse Core Ops, SparseCore 0:
  9.9 30.4 all-gather.15
  42.3 27.7 all-gather.17
  275.9 47.0 all-gather.11
  325.0 85.9 all-gather.13
  414.2 49.5 reduce-scatter.8
  467.1 51.1 reduce-scatter.10
